TPU v7x, 32 devices: a whole 2x2x4 slice. The times are simulated.
32 devices in a mesh: groups: 2 (over y), seq: 4 (over z), mp: 2 (over x), section: 2 (over core).
Axes of the slice: x: 2, y: 2, z: 4, core: 2. Of those that a mesh axis runs over, the one named last changes fastest.
Arguments:
- features: bfloat16 [4, 512, 8192], P(('groups', 'section'), 'mp', 'seq'), parts along dimension 0, may hold values from -6 to 6
- alpha: float32 [512], P('mp'), may hold values from 0.5 to 2
- conv_weight: bfloat16 [1024, 32, 16], P('mp'), may hold values from -0.25 to 0.25
- qkv_weight: bfloat16 [1024, 3, 1024], P(None, None, 'mp'), may hold values from -1 to 1
- readout: float32 [1024], P('mp'), may hold values from -4 to 4
- offsets: int32 [4], P(('groups', 'section')), parts along dimension 0, may hold values from 0 to 14479
- pairs: int32 [8, 2], P('groups'), parts along dimension 0, may hold values from 0 to 1
- labels: int32 [8], P('groups'), parts along dimension 0, may hold values from 0 to 1
Outputs:
- grads: bfloat16 [3, 4, 1024, 1024], P(None, ('groups', 'section'), 'seq', 'mp'), parts along dimension 1
- rewards: float32 [4], P('groups'), parts along dimension 0
- loss: float32 [2], P('groups'), parts along dimension 0
There are 2 independent parts, one for each index of `groups`. A program takes and returns all parts, laid end to end along the dimension named above; an argument that names none is the same for every part. Nothing has to cross between parts.
All inputs are finite; a program needn't handle non-finite values.
Results may differ from a plain program's by a relative error of at most 0.017.
Values may be sent and summed in bfloat16 or wider, within the bound.
A program may use at most 64 MiB of HBM per device.

v0:
```python
import math
import jax
import jax.numpy as jnp
from jax import lax
from jax.sharding import PartitionSpec as P

D = 1024
HD = 64
EPS = 1e-06
BASE = 10000.0


def padded_2(block, sides, width):
    for axis, dim in sides:
        count = lax.axis_size(axis)
        forward = [(i, i + 1) for i in range(count - 1)]
        backward = [(target, source) for source, target in forward]
        low = lax.ppermute(
            lax.slice_in_dim(block, block.shape[dim] - width, None, axis=dim), axis, forward
        )
        high = lax.ppermute(lax.slice_in_dim(block, 0, width, axis=dim), axis, backward)
        block = jnp.concatenate([low, block, high], axis=dim)
    return block


def position_table(positions, feature_ids, width):
    pair_ids = (feature_ids // 2).astype(jnp.float32)
    freqs = jnp.exp(pair_ids * (-2.0 * math.log(BASE) / width))
    angle = positions.astype(jnp.float32)[..., None] * freqs
    return jnp.where(feature_ids % 2 == 0, jnp.sin(angle), jnp.cos(angle))


def local(features, alpha, conv_weight, qkv_weight, readout, offsets, pairs, labels):
    f32 = jnp.float32
    bf16 = jnp.bfloat16
    cand, chans, samples = features.shape
    local_width = conv_weight.shape[0]
    per_group = conv_weight.shape[1]
    kern = conv_weight.shape[2]
    stride = kern // 2
    frames_dev = samples // stride
    groups_here = chans // per_group
    heads_here = local_width // HD
    raw = features.astype(f32)
    slope = alpha[None, :, None]
    act = (raw + jnp.sin(slope * raw) ** 2 / slope).astype(bf16)
    padded = padded_2(act, (("seq", 2),), stride // 2)
    blocks = padded.reshape(cand, groups_here, per_group, frames_dev + 1, stride).transpose(
        0, 1, 3, 2, 4
    )
    patches = jnp.concatenate([blocks[:, :, :-1], blocks[:, :, 1:]], axis=-1).reshape(
        cand, groups_here, frames_dev, per_group * kern
    )
    kernel = conv_weight.reshape(groups_here, local_width // groups_here, per_group * kern)
    frames = jnp.einsum("cgfk,gok->cfgo", patches, kernel, preferred_element_type=f32).reshape(
        cand, frames_dev, local_width
    )
    slice_id = lax.axis_index("seq")
    part_id = lax.axis_index("mp")
    positions = (
        offsets[:, None] + slice_id * frames_dev + jnp.arange(frames_dev, dtype=jnp.int32)[None, :]
    )
    feature_ids = part_id * local_width + jnp.arange(local_width, dtype=jnp.int32)
    resid = (frames + position_table(positions, feature_ids, D)).astype(bf16)
    whole = lax.all_gather(resid, "mp", axis=2, tiled=True)
    squares = jnp.mean(jnp.square(whole.astype(f32)), axis=-1)
    projected = jnp.einsum("cfd,dtk->cftk", whole, qkv_weight, preferred_element_type=f32)
    qkv = (projected * lax.rsqrt(squares + EPS)[:, :, None, None]).astype(bf16)
    query = qkv[:, :, 0]
    keys, values = (
        lax.all_gather(qkv[:, :, 1], "seq", axis=1, tiled=True),
        lax.all_gather(qkv[:, :, 2], "seq", axis=1, tiled=True),
    )
    total = keys.shape[1]
    block = min(512, total)
    count_blocks = total // block
    scale = 1.0 / math.sqrt(HD)
    query4 = query.reshape(cand, frames_dev, heads_here, HD)

    def key_slice(source, start, size):
        return lax.dynamic_slice_in_dim(source, start, size, 1).reshape(cand, size, heads_here, HD)

    def scores_for(start, size):
        return (
            jnp.einsum(
                "cfhe,ckhe->chfk", query4, key_slice(keys, start, size), preferred_element_type=f32
            )
            * scale
        )

    def stat_step(carry, index):
        peak_now, mass_now = carry
        score = scores_for(index * block, block)
        fresh = jnp.maximum(peak_now, jnp.max(score, axis=-1))
        mass_now = mass_now * jnp.exp(peak_now - fresh) + jnp.sum(
            jnp.exp(score - fresh[..., None]), axis=-1
        )
        return ((fresh, mass_now), None)

    start_peak = jnp.full((cand, heads_here, frames_dev), -jnp.inf, f32)
    (peak, mass), _ = lax.scan(
        stat_step, (start_peak, jnp.zeros_like(start_peak)), jnp.arange(count_blocks)
    )

    def weights_for(start, size):
        return jnp.exp(scores_for(start, size) - peak[..., None]) / mass[..., None]

    def out_step(running, index):
        start = index * block
        prob = weights_for(start, block).astype(bf16)
        running = running + jnp.einsum(
            "chfk,ckhe->cfhe", prob, key_slice(values, start, block), preferred_element_type=f32
        )
        return (running, None)

    attended4, _ = lax.scan(
        out_step, jnp.zeros((cand, frames_dev, heads_here, HD), f32), jnp.arange(count_blocks)
    )
    attended = attended4.reshape(cand, frames_dev, local_width)
    gate = jax.nn.sigmoid(lax.optimization_barrier(resid).astype(f32))
    section_id = lax.axis_index("section")
    all_cands = cand * lax.axis_size("section")
    owner = (
        jnp.arange(all_cands, dtype=jnp.int32)[None, :]
        == (section_id * cand + jnp.arange(cand, dtype=jnp.int32))[:, None]
    ).astype(f32)
    partial_rewards = jnp.sum(attended * gate * readout, axis=(1, 2)) / math.sqrt(total)
    rewards = lax.psum(jnp.sum(owner * partial_rewards[:, None], axis=0), ("seq", "mp", "section"))
    chosen = (pairs[:, :, None] == jnp.arange(all_cands, dtype=jnp.int32)[None, None, :]).astype(
        f32
    )
    paired = jnp.sum(chosen * rewards[None, None, :], axis=-1)
    margin = paired[:, 0] - paired[:, 1]
    target = labels.astype(f32)
    loss = jnp.sum(jax.nn.softplus(margin) - target * margin)
    coeff = jax.nn.sigmoid(margin) - target
    reward_grad = jnp.sum(coeff[:, None] * (chosen[:, 0] - chosen[:, 1]), axis=0)
    own_grad = jnp.sum(owner * reward_grad[None, :], axis=1)
    upstream = (own_grad[:, None, None] * readout * gate).astype(bf16)
    upstream4 = upstream.reshape(cand, frames_dev, heads_here, HD)
    delta = jnp.sum(upstream4.astype(f32) * attended4, axis=-1).transpose(0, 2, 1)

    def backward_block(start, size):
        prob = weights_for(start, size)
        prob_low = prob.astype(bf16)
        dprob = jnp.einsum(
            "cfhe,ckhe->chfk", upstream4, key_slice(values, start, size), preferred_element_type=f32
        )
        dscore = (prob * (dprob - delta[..., None])).astype(bf16)
        dquery = (
            jnp.einsum(
                "chfk,ckhe->cfhe", dscore, key_slice(keys, start, size), preferred_element_type=f32
            )
            * scale
        )
        dkey = jnp.einsum("chfk,cfhe->kche", dscore, query4, preferred_element_type=f32) * scale
        dvalue = jnp.einsum("chfk,cfhe->kche", prob_low, upstream4, preferred_element_type=f32)
        term = jnp.concatenate(
            [dkey.reshape(size, cand, local_width), dvalue.reshape(size, cand, local_width)],
            axis=-1,
        )
        return (dquery, term)

    zero_query = jnp.zeros((cand, frames_dev, heads_here, HD), f32)

    def grad_step(running, index):
        dquery, term = backward_block(index * block, block)
        return (running + dquery, term.astype(bf16))

    grad_query, stored = lax.scan(grad_step, zero_query, jnp.arange(count_blocks))
    stacked = stored.reshape(total, cand, 2 * local_width)
    summed = lax.psum_scatter(
        stacked.astype(f32).astype(jnp.bfloat16), "seq", scatter_dimension=0, tiled=True
    ).astype(jnp.float32)
    grad_key = summed[:, :, :local_width].transpose(1, 0, 2)
    grad_value = summed[:, :, local_width:].transpose(1, 0, 2)
    grads = jnp.stack(
        [grad_query.reshape(cand, frames_dev, local_width), grad_key, grad_value], axis=0
    ).astype(bf16)
    return (grads, rewards, loss.reshape(1))


def solution(mesh):
    placed = (
        P(("groups", "section"), "mp", "seq"),
        P("mp"),
        P("mp", None, None),
        P(None, None, "mp"),
        P("mp"),
        P(("groups", "section")),
        P("groups", None),
        P("groups"),
    )
    return jax.shard_map(
        local,
        mesh=mesh,
        in_specs=placed,
        out_specs=(P(None, ("groups", "section"), "seq", "mp"), P("groups"), P("groups")),
        check_vma=False,
    )
```

profile of v0, /device:TPU:0, one launch (start us, length us, event | category | flops | bytes accessed | tf_op | source)
XLA Modules:
  0.0 278.7 jit_solution(6267920341593110061)
XLA Ops:
  7.2 8.6 %fusion.25 = bf16[1,256,2048]{2,1,0:T(8,128)(2,1)S(1)} fusion(bf16[1,256,2048]{2,1,0:T(8,128)(2,1)} %param.14, f32[256]{0:T(256)} %param.15), kind=kLoop, calls=%fused_computation.40 | loop fusion | flops 3145728 | bytes 2098176 | tf_op jit(solution)/shard_map/convert_element_type | solution.py:46
  17.0 4.9 %collective-permute-start = (bf16[1,256,4]{2,1,0:T(8,128)(2,1)S(1)}, bf16[1,256,4]{2,1,0:T(8,128)(2,1)S(1)}, u32[]{:S(2)}, u32[]{:S(2)}) collective-permute-start(bf16[1,256,4]{2,1,0:T(8,128)(2,1)S(1)} %get-tuple-element.365), channel_id=1, source_target_pairs={{0,4},{4,8},{8,12},{1,5},{5,9},{9,13},{2,6},{6,10},{10,14},{3,7},{... | collective-permute-start | bytes 6152 | tf_op jit(solution)/shard_map/ppermute | solution.py:18
  24.1 2.4 reshape.438
  28.1 3.5 %concatenate.32 = bf16[1,256,2056]{2,1,0:T(8,128)(2,1)} concatenate(bf16[1,256,4]{2,1,0:T(8,128)(2,1)S(1)} %collective-permute-done, bf16[1,256,2048]{2,1,0:T(8,128)(2,1)} %copy-done.5, bf16[1,256,4]{2,1,0:T(8,128)(2,1)S(1)} %collective-permute-done.1), dimensions={2} | concatenate | bytes 2105344 | tf_op jit(solution)/shard_map/concatenate | solution.py:22
  31.6 2.3 copy.41
  33.9 5.8 %reshape.436 = bf16[1,8,32,257,8]{2,1,4,3,0:T(8,128)(2,1)} reshape(bf16[1,256,2056]{1,2,0:T(8,128)(2,1)} %copy.41) | data formatting | bytes 2105344 | tf_op jit(solution)/shard_map/reshape | solution.py:48
  39.7 6.5 %fusion.53 = (bf16[1,8,256,32,8]{3,1,4,2,0:T(8,128)(2,1)}, bf16[1,8,256,32,8]{3,1,4,2,0:T(8,128)(2,1)}) fusion(bf16[1,8,257,32,8]{3,1,4,2,0:T(8,128)(2,1)} %bitcast.233), kind=kLoop, calls=%fused_computation.102 | loop fusion | bytes 4194304 | tf_op jit(solution)/shard_map/slice | solution.py:51
  46.2 7.7 %copy.42 = bf16[1,8,256,32,8]{2,4,3,1,0:T(8,128)(2,1)} copy(bf16[1,8,256,32,8]{3,1,4,2,0:T(8,128)(2,1)} %get-tuple-element.362) | data formatting | bytes 2097152 | tf_op jit(solution)/shard_map/slice | solution.py:51
  53.9 7.7 %copy.43 = bf16[1,8,256,32,8]{2,4,3,1,0:T(8,128)(2,1)} copy(bf16[1,8,256,32,8]{3,1,4,2,0:T(8,128)(2,1)} %get-tuple-element.363) | data formatting | bytes 2097152 | tf_op jit(solution)/shard_map/slice | solution.py:51
  66.9 3.5 %fusion.31 = bf16[1,256,512]{2,1,0:T(8,128)(2,1)S(1)} fusion(f32[1,256,512]{2,1,0:T(8,128)} %copy.46, f32[512]{0:T(512)S(1)} %fusion.36, f32[256]{0:T(256)S(1)} %add_convert_fusion, pred[512]{0:T(512)(128)(4,1)S(1)} %fusion.33), kind=kLoop, calls=%fused_computation.52 | loop fusion | flops 524288 | bytes 790016 | tf_op jit(solution)/shard_map/convert_element_type | solution.py:64
  71.1 7.3 %all_gather.9 = bf16[1,256,1024]{2,1,0:T(8,128)(2,1)S(1)} all-gather(bf16[1,256,512]{2,1,0:T(8,128)(2,1)S(1)} %fusion.31), channel_id=1, replica_groups=mesh['groups'=2,'seq'=4,'mp'=2,'section'=2] {'mp'}, dimensions={2}, use_global_device_ids=true | all-gather | bytes 786432 | tf_op jit(solution)/shard_map/all_gather | solution.py:65
  82.1 28.3 %all-gather.5.cloned.1.call-done = bf16[1,1024,1,512]{3,1,2,0:T(8,128)(2,1)} async-done(((bf16[1,256,1,512]{3,1,2,0:T(8,128)(2,1)}), bf16[1,1024,1,512]{3,1,2,0:T(8,128)(2,1)}) %all-gather.5.cloned.1.call-update) | async-done | bytes 1048592 | tf_op jit(solution)/shard_map/all_gather | solution.py:71
  110.4 2.3 copy.53
  112.6 16.1 %while.37 = (s32[]{:T(128)}, f32[1,8,256]{2,1,0:T(8,128)S(1)}, f32[1,8,256]{2,1,0:T(8,128)S(1)}, s32[2]{0:T(128)S(1)}, bf16[1,1024,512]{1,2,0:T(8,128)(2,1)}, /*...) while((s32[]{:T(128)}, f32[1,8,256]{2,1,0:T(8,128)S(1)}, ...), condition=%wide.region_4.5_spmd.clone, body=%wide.region_1.4_spmd.clone.sunk | while | flops 139470848 | bytes 10330286 | solution.py:101
  115.0 2.7 bitcast_reduce_fusion.2
  117.7 3.0 %fusion.86 = f32[8,256]{1,0:T(8,128)S(1)} fusion(f32[8,512,256]{2,1,0:T(8,128)} %get-tuple-element.514, f32[8,256]{1,0:T(8,128)S(1)} %bitcast.239), kind=kLoop, calls=%fused_computation.3.clone.1 | loop fusion | flops 3143680 | bytes 4210688 | tf_op jit(solution)/shard_map/while/body/eval_jaxpr/reduce_sum | solution.py:95
  123.1 2.7 bitcast_reduce_fusion.2
  125.8 2.9 %fusion.86 = f32[8,256]{1,0:T(8,128)S(1)} fusion(f32[8,512,256]{2,1,0:T(8,128)} %get-tuple-element.514, f32[8,256]{1,0:T(8,128)S(1)} %bitcast.239), kind=kLoop, calls=%fused_computation.3.clone.1 | loop fusion | flops 3143680 | bytes 4210688 | tf_op jit(solution)/shard_map/while/body/eval_jaxpr/reduce_sum | solution.py:95
  128.7 10.6 %all-gather.7.cloned.1.call-done = bf16[1,1024,1,512]{3,1,2,0:T(8,128)(2,1)} async-done(((bf16[1,256,1,512]{3,1,2,0:T(8,128)(2,1)}), bf16[1,1024,1,512]{3,1,2,0:T(8,128)(2,1)}) %all-gather.7.cloned.1.call-update) | async-done | bytes 1048592 | tf_op jit(solution)/shard_map/all_gather | solution.py:72
  139.4 2.3 copy.54
  141.7 13.9 %while.38 = (s32[]{:T(128)}, f32[1,256,8,64]{1,3,2,0:T(8,128)}, s32[2]{0:T(128)S(1)}, bf16[1,1024,512]{1,2,0:T(8,128)(2,1)}, bf16[1,1024,512]{1,2,0:T(8,128)(2,1...) while((s32[]{:T(128)}, f32[1,256,8,64]{1,3,2,0:T(8,128)}, ...), condition=%wide.region_6.7_spmd.clone, body=%wide.region_5.6_spmd.clone.sunk | while | flops 272891904 | bytes 4473021 | solution.py:116
  142.9 2.3 constant_dynamic-slice_fusion.9
  145.2 3.4 %fusion.90 = f32[1,256,8,64]{1,3,2,0:T(8,128)} fusion(bf16[512,8,64]{0,2,1:T(8,128)(2,1)} %bitcast.236, bf16[512,8,64]{0,2,1:T(8,128)(2,1)} %bitcast.235, f32[8,256]{1,0:T(8,128)S(1)} %bitcast.249, f32[8,256]{1,0:T(8,128)S(1)} %bitcast.245, f32[1,256,8,64]{1,3,2,0:T(8,128)} %get-tuple-element.581, ...), kind=kOutput, calls=%fused_computation.13.clone.1 | convolution fusion | flops 272891904 | bytes 2375681 | tf_op jit(solution)/shard_map/while/body/eval_jaxpr/chfk,ckhe->cfhe/dot_general | solution.py:111
  149.8 2.3 constant_dynamic-slice_fusion.9
  152.0 3.6 %fusion.90 = f32[1,256,8,64]{1,3,2,0:T(8,128)} fusion(bf16[512,8,64]{0,2,1:T(8,128)(2,1)} %bitcast.236, bf16[512,8,64]{0,2,1:T(8,128)(2,1)} %bitcast.235, f32[8,256]{1,0:T(8,128)S(1)} %bitcast.249, f32[8,256]{1,0:T(8,128)S(1)} %bitcast.245, f32[1,256,8,64]{1,3,2,0:T(8,128)} %get-tuple-element.581, ...), kind=kOutput, calls=%fused_computation.13.clone.1 | convolution fusion | flops 272891904 | bytes 2375681 | tf_op jit(solution)/shard_map/while/body/eval_jaxpr/chfk,ckhe->cfhe/dot_general | solution.py:111
  160.3 31.9 %psum.7 = f32[2]{0:T(128)S(1)} all-reduce(f32[2]{0:T(128)S(1)} %compare_select_fusion.2), channel_id=1, replica_groups=mesh['groups'=2,'seq'=4,'mp'=2,'section'=2] {'seq','mp','section'}, use_global_device_ids=true, to_apply=%region_8.9 | all-reduce | flops 2 | bytes 16 | tf_op jit(solution)/shard_map/psum | solution.py:128
  198.3 25.0 %while.39 = (s32[]{:T(128)}, f32[1,256,8,64]{1,3,2,0:T(8,128)}, bf16[2,512,1,1024]{1,3,2,0:T(8,128)(2,1)}, s32[2]{0:T(128)S(1)}, bf16[1,1024,512]{1,2,0:T(8,128)...) while((s32[]{:T(128)}, f32[1,256,8,64]{1,3,2,0:T(8,128)}, ...), condition=%wide.region_14.15_spmd.clone, body=%wide.region_13.14_spmd.clone.sunk | while | flops 681705472 | bytes 39346984 | solution.py:170
  207.7 3.0 %fusion.101 = f32[1,256,8,64]{1,3,2,0:T(8,128)} fusion(bf16[512,8,64]{0,2,1:T(8,128)(2,1)} %bitcast.227, bf16[8,512,256]{2,1,0:T(8,128)(2,1)} %copy-done.1, f32[1,256,8,64]{1,3,2,0:T(8,128)} %get-tuple-element.620, pred[]{:T(512)S(6)} %compare.19), kind=kOutput, calls=%fused_computation.27.clone.1 | convolution fusion | flops 134610944 | bytes 3670017 | tf_op jit(solution)/shard_map/while/body/eval_jaxpr/chfk,ckhe->cfhe/dot_general | solution.py:151
  220.2 3.1 %fusion.101 = f32[1,256,8,64]{1,3,2,0:T(8,128)} fusion(bf16[512,8,64]{0,2,1:T(8,128)(2,1)} %bitcast.227, bf16[8,512,256]{2,1,0:T(8,128)(2,1)} %copy-done.1, f32[1,256,8,64]{1,3,2,0:T(8,128)} %get-tuple-element.620, pred[]{:T(512)S(6)} %compare.19), kind=kOutput, calls=%fused_computation.27.clone.1 | convolution fusion | flops 134610944 | bytes 3670017 | tf_op jit(solution)/shard_map/while/body/eval_jaxpr/chfk,ckhe->cfhe/dot_general | solution.py:151
  223.3 3.3 %copy.58 = bf16[2,1,128,8,512]{4,3,0,2,1:T(8,128)(2,1)} copy(bf16[2,1,128,8,512]{4,3,2,1,0:T(8,128)(2,1)} %bitcast.70) | data formatting | bytes 4194304 | tf_op jit(solution)/shard_map/reshape | solution.py:171
  227.7 40.2 %reduce-scatter.2.cloned.1.call-done = bf16[256,1,1024]{0,2,1:T(8,128)(2,1)} async-done(((bf16[1024,1,1024]{0,2,1:T(8,128)(2,1)}), bf16[256,1,1024]{0,2,1:T(8,128)(2,1)}) %reduce-scatter.2.cloned.1.call-update) | async-done | bytes 524304 | tf_op jit(solution)/shard_map/reduce_scatter | solution.py:172
  269.9 2.3 copy.56
  (100 shorter events, 49.0 us)
Async XLA Ops:
  7.2 71.4 %copy-start = (bf16[1024,3,512]{2,0,1:T(8,128)(2,1)S(1)}, bf16[1024,3,512]{2,0,1:T(8,128)(2,1)}, u32[]{:S(2)}) copy-start(bf16[1024,3,512]{2,0,1:T(8,128)(2,1)} %param.17) | copy-start | bytes 9437188
  7.2 103.2 %all-gather.5.cloned.1.call-start = ((), (), s32[]{:S(2)}) async-start(), calls=%async_computation.2 | async-start | bytes 1310720 | tf_op jit(solution)/shard_map/all_gather | solution.py:71
  15.8 1.0 copy-start.5
  17.0 9.6 %collective-permute-start = (bf16[1,256,4]{2,1,0:T(8,128)(2,1)S(1)}, bf16[1,256,4]{2,1,0:T(8,128)(2,1)S(1)}, u32[]{:S(2)}, u32[]{:S(2)}) collective-permute-start(bf16[1,256,4]{2,1,0:T(8,128)(2,1)S(1)} %get-tuple-element.365), channel_id=1, source_target_pairs={{0,4},{4,8},{8,12},{1,5},{5,9},{9,13},{2,6},{6,10},{10,14},{3,7},{... | collective-permute-start | bytes 6152 | tf_op jit(solution)/shard_map/ppermute | solution.py:18
  21.9 6.2 %collective-permute-start.1 = (bf16[1,256,4]{2,1,0:T(8,128)(2,1)S(1)}, bf16[1,256,4]{2,1,0:T(8,128)(2,1)S(1)}, u32[]{:S(2)}, u32[]{:S(2)}) collective-permute-start(bf16[1,256,4]{2,1,0:T(8,128)(2,1)S(1)} %get-tuple-element.364), channel_id=1, source_target_pairs={{4,0},{8,4},{12,8},{5,1},{9,5},{13,9},{6,2},{10,6},{14,10},{7,3},{... | collective-permute-start | bytes 6152 | tf_op jit(solution)/shard_map/ppermute | solution.py:21
  61.7 1.9 copy-start.6
  70.4 0.7 copy-start.7
  78.6 2.1 copy-start.9
  80.6 58.8 %all-gather.7.cloned.1.call-start = ((), (), s32[]{:S(2)}) async-start(), calls=%async_computation.3 | async-start | bytes 1310720 | tf_op jit(solution)/shard_map/all_gather | solution.py:72
  81.8 186.0 %reduce-scatter.2.cloned.1.call-start = ((), (), s32[]{:S(2)}) async-start(), calls=%async_computation.1 | async-start | bytes 2621440 | tf_op jit(solution)/shard_map/reduce_scatter | solution.py:172
  141.7 16.1 %copy-start.8 = (f32[512]{0:T(512)S(1)}, f32[512]{0:T(512)}, u32[]{:S(2)}) copy-start(f32[512]{0:T(512)} %param.18) | copy-start | bytes 6148
  141.7 50.6 %copy-start.10 = (s32[4]{0:T(128)S(1)}, s32[4]{0:T(128)}, u32[]{:S(2)}) copy-start(s32[4]{0:T(128)} %param.21) | copy-start | bytes 52
  155.6 38.7 %copy-start.3 = (bf16[1,256,8,64]{1,3,2,0:T(8,128)(2,1)}, bf16[1,256,8,64]{1,3,2,0:T(8,128)(2,1)S(1)}, u32[]{:S(2)}) copy-start(bf16[1,256,8,64]{1,3,2,0:T(8,128)(2,1)S(1)} %get-tuple-element.656) | copy-start | bytes 786436
  192.2 6.1 %copy-start.11 = (f32[2]{0:T(128)}, f32[2]{0:T(128)S(1)}, u32[]{:S(2)}) copy-start(f32[2]{0:T(128)S(1)} %psum.7) | copy-start | bytes 28
  200.8 2.2 copy-start.2
  203.0 2.1 copy-start.4
  203.8 1.3 copy-start.1
  213.3 2.2 copy-start.2
  215.5 2.1 copy-start.4
  216.3 1.3 copy-start.1
Sparse Core Ops, SparseCore 0:
  80.7 29.6 all-gather.4
  111.9 27.4 all-gather.6
  226.7 41.0 reduce-scatter.1
where the time goes:
time: 280 us; the launch traced here: 279 us
  waiting for transfers between devices  80.7 us (29%)
  local copies, waits for them, and re-layouts  71.9 us (26%)
  blocking collectives  39.2 us (14%)
  other arithmetic  31.1 us (11%)
  matrix products  29.7 us (11%)
  between operations  15.3 us (5%)
  starting transfers between devices  6.74 us (2%)
  loops' own time  4.08 us (1%)
    reduce_scatter x1, waiting for transfers between devices, local(): lax.psum_scatter(stacked.astype(f32).astype(jnp.bfloat16), 'seq', scatter...  40.2 us
    psum x1, blocking collectives, local(): lax.psum(jnp.sum(owner * partial_rewards[:, None], axis=0), ('seq', 'mp',...  31.9 us
    all_gather x1, waiting for transfers between devices, local(): lax.all_gather(qkv[:, :, 1], 'seq', axis=1, tiled=True)  28.3 us
    slice x2, local copies, waits for them, and re-layouts, local(): blocks[:, :, :-1]  14.2 us
    all_gather x1, waiting for transfers between devices, local(): lax.all_gather(qkv[:, :, 2], 'seq', axis=1, tiled=True)  10.6 us
    dot_general x4, matrix products, scores_for(): jnp.einsum('cfhe,ckhe->chfk', query4, key_slice(keys, start, size), prefe...  9.74 us
    dynamic_slice x6, local copies, waits for them, and re-layouts, key_slice(): lax.dynamic_slice_in_dim(source, start, size, 1)  9.22 us
    unnamed x21, local copies, waits for them, and re-layouts  8.64 us
  transfers between devices with their start and end apart: 5, of which 4 were waited for; matrix products, arithmetic and copies ran while one was open for 8% of the time, Pallas kernels for 0%

commit v1 on v0

--- a/solution.py
+++ b/solution.py
@@ -125,7 +125,9 @@
         == (section_id * cand + jnp.arange(cand, dtype=jnp.int32))[:, None]
     ).astype(f32)
     partial_rewards = jnp.sum(attended * gate * readout, axis=(1, 2)) / math.sqrt(total)
-    rewards = lax.psum(jnp.sum(owner * partial_rewards[:, None], axis=0), ("seq", "mp", "section"))
+    own = jnp.sum(owner * partial_rewards[:, None], axis=0)
+    parts = lax.all_gather(own, ("seq", "mp", "section"))
+    rewards = jnp.sum(parts, axis=0)
     chosen = (pairs[:, :, None] == jnp.arange(all_cands, dtype=jnp.int32)[None, None, :]).astype(
         f32
     )

time: 280 us -> 268 us (0.957)
  blocking collectives: 39.2 us -> 27.1 us
    psum x1 -> x0, blocking collectives: 31.9 us -> none  [local(): lax.psum(jnp.sum(owner * partial_rewards[:, None], axis=0), ('seq', 'mp',...]
    all_gather x0 -> x1, blocking collectives: none -> 19.8 us  [local(): parts = lax.all_gather(own, ('seq', 'mp', 'section'))]
where the time goes in v1:
time: 268 us; the launch traced here: 267 us
  waiting for transfers between devices  80.7 us (30%)
  local copies, waits for them, and re-layouts  71.9 us (27%)
  other arithmetic  31.2 us (12%)
  matrix products  29.7 us (11%)
  blocking collectives  27.1 us (10%)
  between operations  15.3 us (6%)
  starting transfers between devices  6.74 us (3%)
  loops' own time  4.08 us (2%)
    reduce_scatter x1, waiting for transfers between devices, local(): lax.psum_scatter(stacked.astype(f32).astype(jnp.bfloat16), 'seq', scatter...  40.2 us
    all_gather x1, waiting for transfers between devices, local(): lax.all_gather(qkv[:, :, 1], 'seq', axis=1, tiled=True)  28.3 us
    all_gather x1, blocking collectives, local(): parts = lax.all_gather(own, ('seq', 'mp', 'section'))  19.8 us
    slice x2, local copies, waits for them, and re-layouts, local(): blocks[:, :, :-1]  14.2 us
    all_gather x1, waiting for transfers between devices, local(): lax.all_gather(qkv[:, :, 2], 'seq', axis=1, tiled=True)  10.6 us
    dot_general x4, matrix products, scores_for(): jnp.einsum('cfhe,ckhe->chfk', query4, key_slice(keys, start, size), prefe...  9.74 us
    dynamic_slice x6, local copies, waits for them, and re-layouts, key_slice(): lax.dynamic_slice_in_dim(source, start, size, 1)  9.22 us
    unnamed x21, local copies, waits for them, and re-layouts  8.64 us
  transfers between devices with their start and end apart: 5, of which 4 were waited for; matrix products, arithmetic and copies ran while one was open for 8% of the time, Pallas kernels for 0%

profile of v1, /device:TPU:0, one launch (start us, length us, event | category | flops | bytes accessed | tf_op | source)
XLA Modules:
  0.0 266.6 jit_solution(14954498086270851896)
XLA Ops:
  7.2 8.6 %fusion.25 = bf16[1,256,2048]{2,1,0:T(8,128)(2,1)S(1)} fusion(bf16[1,256,2048]{2,1,0:T(8,128)(2,1)} %param.14, f32[256]{0:T(256)} %param.15), kind=kLoop, calls=%fused_computation.40 | loop fusion | flops 3145728 | bytes 2098176 | tf_op jit(solution)/shard_map/convert_element_type | solution.py:46
  17.0 4.9 %collective-permute-start = (bf16[1,256,4]{2,1,0:T(8,128)(2,1)S(1)}, bf16[1,256,4]{2,1,0:T(8,128)(2,1)S(1)}, u32[]{:S(2)}, u32[]{:S(2)}) collective-permute-start(bf16[1,256,4]{2,1,0:T(8,128)(2,1)S(1)} %get-tuple-element.365), channel_id=1, source_target_pairs={{0,4},{4,8},{8,12},{1,5},{5,9},{9,13},{2,6},{6,10},{10,14},{3,7},{... | collective-permute-start | bytes 6152 | tf_op jit(solution)/shard_map/ppermute | solution.py:18
  24.1 2.4 reshape.448
  28.1 3.5 %concatenate.32 = bf16[1,256,2056]{2,1,0:T(8,128)(2,1)} concatenate(bf16[1,256,4]{2,1,0:T(8,128)(2,1)S(1)} %collective-permute-done, bf16[1,256,2048]{2,1,0:T(8,128)(2,1)} %copy-done.5, bf16[1,256,4]{2,1,0:T(8,128)(2,1)S(1)} %collective-permute-done.1), dimensions={2} | concatenate | bytes 2105344 | tf_op jit(solution)/shard_map/concatenate | solution.py:22
  31.6 2.3 copy.41
  33.9 5.8 %reshape.446 = bf16[1,8,32,257,8]{2,1,4,3,0:T(8,128)(2,1)} reshape(bf16[1,256,2056]{1,2,0:T(8,128)(2,1)} %copy.41) | data formatting | bytes 2105344 | tf_op jit(solution)/shard_map/reshape | solution.py:48
  39.7 6.5 %fusion.54 = (bf16[1,8,256,32,8]{3,1,4,2,0:T(8,128)(2,1)}, bf16[1,8,256,32,8]{3,1,4,2,0:T(8,128)(2,1)}) fusion(bf16[1,8,257,32,8]{3,1,4,2,0:T(8,128)(2,1)} %bitcast.235), kind=kLoop, calls=%fused_computation.103 | loop fusion | bytes 4194304 | tf_op jit(solution)/shard_map/slice | solution.py:51
  46.2 7.7 %copy.42 = bf16[1,8,256,32,8]{2,4,3,1,0:T(8,128)(2,1)} copy(bf16[1,8,256,32,8]{3,1,4,2,0:T(8,128)(2,1)} %get-tuple-element.362) | data formatting | bytes 2097152 | tf_op jit(solution)/shard_map/slice | solution.py:51
  53.9 7.7 %copy.43 = bf16[1,8,256,32,8]{2,4,3,1,0:T(8,128)(2,1)} copy(bf16[1,8,256,32,8]{3,1,4,2,0:T(8,128)(2,1)} %get-tuple-element.363) | data formatting | bytes 2097152 | tf_op jit(solution)/shard_map/slice | solution.py:51
  66.9 3.5 %fusion.31 = bf16[1,256,512]{2,1,0:T(8,128)(2,1)S(1)} fusion(f32[1,256,512]{2,1,0:T(8,128)} %copy.46, f32[512]{0:T(512)S(1)} %fusion.36, f32[256]{0:T(256)S(1)} %add_convert_fusion, pred[512]{0:T(512)(128)(4,1)S(1)} %fusion.33), kind=kLoop, calls=%fused_computation.52 | loop fusion | flops 524288 | bytes 790016 | tf_op jit(solution)/shard_map/convert_element_type | solution.py:64
  71.1 7.3 %all_gather.13 = bf16[1,256,1024]{2,1,0:T(8,128)(2,1)S(1)} all-gather(bf16[1,256,512]{2,1,0:T(8,128)(2,1)S(1)} %fusion.31), channel_id=1, replica_groups=mesh['groups'=2,'seq'=4,'mp'=2,'section'=2] {'mp'}, dimensions={2}, use_global_device_ids=true | all-gather | bytes 786432 | tf_op jit(solution)/shard_map/all_gather | solution.py:65
  82.1 28.3 %all-gather.6.cloned.1.call-done = bf16[1,1024,1,512]{3,1,2,0:T(8,128)(2,1)} async-done(((bf16[1,256,1,512]{3,1,2,0:T(8,128)(2,1)}), bf16[1,1024,1,512]{3,1,2,0:T(8,128)(2,1)}) %all-gather.6.cloned.1.call-update) | async-done | bytes 1048592 | tf_op jit(solution)/shard_map/all_gather | solution.py:71
  110.4 2.3 copy.53
  112.6 16.1 %while.37 = (s32[]{:T(128)}, f32[1,8,256]{2,1,0:T(8,128)S(1)}, f32[1,8,256]{2,1,0:T(8,128)S(1)}, s32[2]{0:T(128)S(1)}, bf16[1,1024,512]{1,2,0:T(8,128)(2,1)}, /*...) while((s32[]{:T(128)}, f32[1,8,256]{2,1,0:T(8,128)S(1)}, ...), condition=%wide.region_4.5_spmd.clone, body=%wide.region_1.4_spmd.clone.sunk | while | flops 139470848 | bytes 10330286 | solution.py:101
  115.0 2.7 %bitcast_reduce_fusion.2 = (f32[8,256]{1,0:T(8,128)S(1)}, f32[8,512,256]{2,1,0:T(8,128)}) fusion(bf16[512,8,64]{0,2,1:T(8,128)(2,1)S(1)} %bitcast.230, bf16[1,256,8,64]{1,3,2,0:T(8,128)(2,1)S(1)} %get-tuple-element.563), kind=kOutput, calls=%fused_computation.1.clone.1 | convolution fusion | flops 136312832 | bytes 4988928 | tf_op jit(solution)/shard_map/while/body/eval_jaxpr/cfhe,ckhe->chfk/dot_general | solution.py:85
  117.7 3.0 %fusion.87 = f32[8,256]{1,0:T(8,128)S(1)} fusion(f32[8,512,256]{2,1,0:T(8,128)} %get-tuple-element.514, f32[8,256]{1,0:T(8,128)S(1)} %bitcast.241), kind=kLoop, calls=%fused_computation.3.clone.1 | loop fusion | flops 3143680 | bytes 4210688 | tf_op jit(solution)/shard_map/while/body/eval_jaxpr/reduce_sum | solution.py:95
  123.1 2.7 %bitcast_reduce_fusion.2 = (f32[8,256]{1,0:T(8,128)S(1)}, f32[8,512,256]{2,1,0:T(8,128)}) fusion(bf16[512,8,64]{0,2,1:T(8,128)(2,1)S(1)} %bitcast.230, bf16[1,256,8,64]{1,3,2,0:T(8,128)(2,1)S(1)} %get-tuple-element.563), kind=kOutput, calls=%fused_computation.1.clone.1 | convolution fusion | flops 136312832 | bytes 4988928 | tf_op jit(solution)/shard_map/while/body/eval_jaxpr/cfhe,ckhe->chfk/dot_general | solution.py:85
  125.8 2.9 %fusion.87 = f32[8,256]{1,0:T(8,128)S(1)} fusion(f32[8,512,256]{2,1,0:T(8,128)} %get-tuple-element.514, f32[8,256]{1,0:T(8,128)S(1)} %bitcast.241), kind=kLoop, calls=%fused_computation.3.clone.1 | loop fusion | flops 3143680 | bytes 4210688 | tf_op jit(solution)/shard_map/while/body/eval_jaxpr/reduce_sum | solution.py:95
  128.7 10.6 %all-gather.8.cloned.1.call-done = bf16[1,1024,1,512]{3,1,2,0:T(8,128)(2,1)} async-done(((bf16[1,256,1,512]{3,1,2,0:T(8,128)(2,1)}), bf16[1,1024,1,512]{3,1,2,0:T(8,128)(2,1)}) %all-gather.8.cloned.1.call-update) | async-done | bytes 1048592 | tf_op jit(solution)/shard_map/all_gather | solution.py:72
  139.4 2.3 copy.54
  141.7 13.9 %while.38 = (s32[]{:T(128)}, f32[1,256,8,64]{1,3,2,0:T(8,128)}, s32[2]{0:T(128)S(1)}, bf16[1,1024,512]{1,2,0:T(8,128)(2,1)}, bf16[1,1024,512]{1,2,0:T(8,128)(2,1...) while((s32[]{:T(128)}, f32[1,256,8,64]{1,3,2,0:T(8,128)}, ...), condition=%wide.region_6.7_spmd.clone, body=%wide.region_5.6_spmd.clone.sunk | while | flops 272891904 | bytes 4473021 | solution.py:116
  142.9 2.3 constant_dynamic-slice_fusion.9
  145.2 3.4 %fusion.91 = f32[1,256,8,64]{1,3,2,0:T(8,128)} fusion(bf16[512,8,64]{0,2,1:T(8,128)(2,1)} %bitcast.238, bf16[512,8,64]{0,2,1:T(8,128)(2,1)} %bitcast.237, f32[8,256]{1,0:T(8,128)S(1)} %bitcast.251, f32[8,256]{1,0:T(8,128)S(1)} %bitcast.247, f32[1,256,8,64]{1,3,2,0:T(8,128)} %get-tuple-element.581, ...), kind=kOutput, calls=%fused_computation.13.clone.1 | convolution fusion | flops 272891904 | bytes 2375681 | tf_op jit(solution)/shard_map/while/body/eval_jaxpr/chfk,ckhe->cfhe/dot_general | solution.py:111
  149.8 2.3 constant_dynamic-slice_fusion.9
  152.0 3.6 %fusion.91 = f32[1,256,8,64]{1,3,2,0:T(8,128)} fusion(bf16[512,8,64]{0,2,1:T(8,128)(2,1)} %bitcast.238, bf16[512,8,64]{0,2,1:T(8,128)(2,1)} %bitcast.237, f32[8,256]{1,0:T(8,128)S(1)} %bitcast.251, f32[8,256]{1,0:T(8,128)S(1)} %bitcast.247, f32[1,256,8,64]{1,3,2,0:T(8,128)} %get-tuple-element.581, ...), kind=kOutput, calls=%fused_computation.13.clone.1 | convolution fusion | flops 272891904 | bytes 2375681 | tf_op jit(solution)/shard_map/while/body/eval_jaxpr/chfk,ckhe->cfhe/dot_general | solution.py:111
  160.3 19.8 %all-gather.2 = f32[16,1,2]{2,1,0:T(1,128)S(1)} all-gather(f32[1,1,2]{2,1,0:T(1,128)S(1)} %fusion.45), channel_id=1, replica_groups=mesh['groups'=2,'seq'=4,'mp'=2,'section'=2] {'seq','mp','section'}, dimensions={0}, use_global_device_ids=true | all-gather | bytes 136 | tf_op jit(solution)/shard_map/all_gather | solution.py:129
  186.2 25.0 %while.39 = (s32[]{:T(128)}, f32[1,256,8,64]{1,3,2,0:T(8,128)}, bf16[2,512,1,1024]{1,3,2,0:T(8,128)(2,1)}, s32[2]{0:T(128)S(1)}, bf16[1,1024,512]{1,2,0:T(8,128)...) while((s32[]{:T(128)}, f32[1,256,8,64]{1,3,2,0:T(8,128)}, ...), condition=%wide.region_14.15_spmd.clone, body=%wide.region_13.14_spmd.clone.sunk | while | flops 681705472 | bytes 39346984 | solution.py:172
  195.6 3.0 %fusion.102 = f32[1,256,8,64]{1,3,2,0:T(8,128)} fusion(bf16[512,8,64]{0,2,1:T(8,128)(2,1)} %bitcast.229, bf16[8,512,256]{2,1,0:T(8,128)(2,1)} %copy-done.1, f32[1,256,8,64]{1,3,2,0:T(8,128)} %get-tuple-element.620, pred[]{:T(512)S(6)} %compare.19), kind=kOutput, calls=%fused_computation.27.clone.1 | convolution fusion | flops 134610944 | bytes 3670017 | tf_op jit(solution)/shard_map/while/body/eval_jaxpr/chfk,ckhe->cfhe/dot_general | solution.py:153
  208.1 3.1 %fusion.102 = f32[1,256,8,64]{1,3,2,0:T(8,128)} fusion(bf16[512,8,64]{0,2,1:T(8,128)(2,1)} %bitcast.229, bf16[8,512,256]{2,1,0:T(8,128)(2,1)} %copy-done.1, f32[1,256,8,64]{1,3,2,0:T(8,128)} %get-tuple-element.620, pred[]{:T(512)S(6)} %compare.19), kind=kOutput, calls=%fused_computation.27.clone.1 | convolution fusion | flops 134610944 | bytes 3670017 | tf_op jit(solution)/shard_map/while/body/eval_jaxpr/chfk,ckhe->cfhe/dot_general | solution.py:153
  211.2 3.3 %copy.58 = bf16[2,1,128,8,512]{4,3,0,2,1:T(8,128)(2,1)} copy(bf16[2,1,128,8,512]{4,3,2,1,0:T(8,128)(2,1)} %bitcast.71) | data formatting | bytes 4194304 | tf_op jit(solution)/shard_map/reshape | solution.py:173
  215.6 40.2 %reduce-scatter.2.cloned.1.call-done = bf16[256,1,1024]{0,2,1:T(8,128)(2,1)} async-done(((bf16[1024,1,1024]{0,2,1:T(8,128)(2,1)}), bf16[256,1,1024]{0,2,1:T(8,128)(2,1)}) %reduce-scatter.2.cloned.1.call-update) | async-done | bytes 524304 | tf_op jit(solution)/shard_map/reduce_scatter | solution.py:174
  257.8 2.3 copy.56
  (101 shorter events, 49.0 us)
Async XLA Ops:
  7.2 71.4 %copy-start = (bf16[1024,3,512]{2,0,1:T(8,128)(2,1)S(1)}, bf16[1024,3,512]{2,0,1:T(8,128)(2,1)}, u32[]{:S(2)}) copy-start(bf16[1024,3,512]{2,0,1:T(8,128)(2,1)} %param.17) | copy-start | bytes 9437188
  7.2 103.2 %all-gather.6.cloned.1.call-start = ((), (), s32[]{:S(2)}) async-start(), calls=%async_computation.2 | async-start | bytes 1310720 | tf_op jit(solution)/shard_map/all_gather | solution.py:71
  15.8 1.0 copy-start.5
  17.0 9.6 %collective-permute-start = (bf16[1,256,4]{2,1,0:T(8,128)(2,1)S(1)}, bf16[1,256,4]{2,1,0:T(8,128)(2,1)S(1)}, u32[]{:S(2)}, u32[]{:S(2)}) collective-permute-start(bf16[1,256,4]{2,1,0:T(8,128)(2,1)S(1)} %get-tuple-element.365), channel_id=1, source_target_pairs={{0,4},{4,8},{8,12},{1,5},{5,9},{9,13},{2,6},{6,10},{10,14},{3,7},{... | collective-permute-start | bytes 6152 | tf_op jit(solution)/shard_map/ppermute | solution.py:18
  21.9 6.2 %collective-permute-start.1 = (bf16[1,256,4]{2,1,0:T(8,128)(2,1)S(1)}, bf16[1,256,4]{2,1,0:T(8,128)(2,1)S(1)}, u32[]{:S(2)}, u32[]{:S(2)}) collective-permute-start(bf16[1,256,4]{2,1,0:T(8,128)(2,1)S(1)} %get-tuple-element.364), channel_id=1, source_target_pairs={{4,0},{8,4},{12,8},{5,1},{9,5},{13,9},{6,2},{10,6},{14,10},{7,3},{... | collective-permute-start | bytes 6152 | tf_op jit(solution)/shard_map/ppermute | solution.py:21
  61.7 1.9 copy-start.6
  70.4 0.7 copy-start.7
  78.6 2.1 copy-start.9
  80.6 58.8 %all-gather.8.cloned.1.call-start = ((), (), s32[]{:S(2)}) async-start(), calls=%async_computation.3 | async-start | bytes 1310720 | tf_op jit(solution)/shard_map/all_gather | solution.py:72
  81.8 174.0 %reduce-scatter.2.cloned.1.call-start = ((), (), s32[]{:S(2)}) async-start(), calls=%async_computation.1 | async-start | bytes 2621440 | tf_op jit(solution)/shard_map/reduce_scatter | solution.py:174
  141.7 16.1 %copy-start.8 = (f32[512]{0:T(512)S(1)}, f32[512]{0:T(512)}, u32[]{:S(2)}) copy-start(f32[512]{0:T(512)} %param.18) | copy-start | bytes 6148
  141.7 38.5 %copy-start.11 = (s32[4]{0:T(128)S(1)}, s32[4]{0:T(128)}, u32[]{:S(2)}) copy-start(s32[4]{0:T(128)} %param.21) | copy-start | bytes 52
  155.6 26.6 %copy-start.3 = (bf16[1,256,8,64]{1,3,2,0:T(8,128)(2,1)}, bf16[1,256,8,64]{1,3,2,0:T(8,128)(2,1)S(1)}, u32[]{:S(2)}) copy-start(bf16[1,256,8,64]{1,3,2,0:T(8,128)(2,1)S(1)} %get-tuple-element.656) | copy-start | bytes 786436
  180.1 6.1 %copy-start.10 = (f32[2]{0:T(128)}, f32[2]{0:T(128)S(1)}, u32[]{:S(2)}) copy-start(f32[2]{0:T(128)S(1)} %reduce_sum.91) | copy-start | bytes 28
  188.8 2.2 copy-start.2
  191.0 2.1 copy-start.4
  191.7 1.3 copy-start.1
  201.2 2.2 copy-start.2
  203.4 2.1 copy-start.4
  204.2 1.3 copy-start.1
Sparse Core Ops, SparseCore 0:
  80.7 29.6 all-gather.5
  111.9 27.4 all-gather.7
  214.6 41.0 reduce-scatter.1
